TPU v7x, 256 devices: a whole 4x4x8 slice. The times are simulated.
256 devices in a mesh: section: 2 (over y_lo), dp: 4 (over y_hi, core), shard: 32 (over x, z).
Axes of the slice: x: 4, y: 4 (y_hi: 2, y_lo: 2; y = y_hi * 2 + y_lo), z: 8, core: 2. Of those that a mesh axis runs over, the one named last changes fastest.
Arguments:
- norm_input: bfloat16 [2, 4, 4096, 3584], P('section', 'dp', 'shard'), may hold values from -6 to 6
- norm_gain: float32 [2, 3584], P('section'), may hold values from 0.1 to 1.9
- branch_grad: bfloat16 [2, 4, 4096, 3584], P('section', 'dp', 'shard'), may hold values from -6 to 6
- residual_grad: bfloat16 [2, 4, 4096, 3584], P('section', 'dp', 'shard'), may hold values from -6 to 6
- down_weight: bfloat16 [2, 14336, 3584], P('section', 'shard'), may hold values from -0.09375 to 0.09375
Outputs:
- boundary_grad: bfloat16 [2, 4, 4096, 3584], P('section', 'dp', 'shard')
- gain_grad: float32 [2, 3584], P('section')
- unit_grads: bfloat16 [2, 4, 4096, 14336], P('section', 'dp', None, 'shard')
All inputs are finite; a program needn't handle non-finite values.
Results may differ from a plain program's by a relative error of at most 0.0049.
Values may be sent and summed in bfloat16 or wider, within the bound.
A program may use at most 128 MiB of HBM per device.

v0:
```python
import jax
import jax.numpy as jnp
from jax import lax
from jax.sharding import Mesh
from jax.sharding import PartitionSpec as P

DP_SHARD = ("dp_0", "dp_1", "shard_0", "shard_1")
SHARD = ("shard_0", "shard_1")
DP = ("dp_0", "dp_1")


epsilon = 1e-05


def one_axis_at_a_time(array, axes):
    for axis in axes:
        array = lax.psum(array, axis)
    return array


def from_partner(block, axis, distance):
    count = lax.axis_size(axis)
    route = []
    for low in range(count):
        high = low | 1 << distance
        if high != low and high < count:
            route += [(low, high), (high, low)]
    return lax.ppermute(block, axis, route)


def norm_backward(inputs, gain_row, branch, residual):
    values = inputs.astype(jnp.float32)
    inverse = lax.rsqrt(jnp.mean(values * values, axis=-1, keepdims=True) + epsilon)
    normed = values * inverse
    upstream = branch.astype(jnp.float32)
    scaled = upstream * gain_row
    project = jnp.mean(scaled * normed, axis=-1, keepdims=True)
    boundary = (residual.astype(jnp.float32) + inverse * (scaled - normed * project)).astype(
        jnp.bfloat16
    )
    return (boundary, jnp.sum(upstream * normed, axis=0))


def per_device(norm_input, norm_gain, branch_grad, residual_grad, down_weight):
    weight = down_weight[0]
    boundary, gain_part = norm_backward(
        norm_input[0, 0], norm_gain[0], branch_grad[0, 0], residual_grad[0, 0]
    )
    gain_total = one_axis_at_a_time(gain_part, DP_SHARD)
    arrived = from_partner(boundary, "section", 0)
    fresh = jnp.einsum(
        "nd,hd->nh",
        lax.all_gather(arrived, SHARD, axis=0, tiled=True),
        weight,
        preferred_element_type=jnp.float32,
    ).astype(jnp.bfloat16)
    gain_grad = gain_total / fresh.shape[0]
    return (boundary[None, None], gain_grad[None], fresh[None, None])


def solution(mesh):
    split = Mesh(
        mesh.devices.reshape(mesh.shape["section"], 2, 2, 4, 8),
        ("section", "dp_0", "dp_1", "shard_0", "shard_1"),
    )
    return jax.shard_map(
        per_device,
        mesh=split,
        in_specs=(
            P("section", DP, SHARD, None),
            P("section", None),
            P("section", DP, SHARD, None),
            P("section", DP, SHARD, None),
            P("section", SHARD, None),
        ),
        out_specs=(
            P("section", DP, SHARD, None),
            P("section", None),
            P("section", DP, None, SHARD),
        ),
        check_vma=False,
    )
```

profile of v0, /device:TPU:16, one launch (start us, length us, event | category | flops | bytes accessed | tf_op | source)
XLA Modules:
  0.0 274.9 jit_solution(16686822337064339081)
XLA Ops:
  7.2 0.0 copy-start
  7.2 0.0 all-gather.2.cloned.1.call-start
  7.2 1.6 fusion.17
  8.8 0.8 reduce
  9.6 0.0 copy-start.1
  9.6 0.0 copy-start.2
  9.6 2.3 fusion.16
  11.9 0.0 copy-done.1
  11.9 0.0 copy-done.2
  11.9 1.8 fusion.11
  13.8 1.4 collective-permute-start
  15.1 20.9 %collective-permute-done = bf16[128,3584]{1,0:T(8,128)(2,1)} collective-permute-done((bf16[128,3584]{1,0:T(8,128)(2,1)S(1)}, bf16[128,3584]{1,0:T(8,128)(2,1)}, u32[]{:S(2)}, u32[]{:S(2)}) %collective-permute-start) | collective-permute-done | bytes 917536 | tf_op jit(solution)/shard_map/ppermute | solution.py:28
  36.1 0.0 all-gather.2.cloned.1.call-update
  36.1 8.3 %psum.28 = f32[3584]{0:T(1024)S(1)} all-reduce(f32[3584]{0:T(1024)S(1)} %get-tuple-element.3), channel_id=1, replica_groups=mesh['section'=2,'dp_0'=2,'dp_1'=2,'shard_0'=4,'shard_1'=8] {'dp_0'}, use_global_device_ids=true, to_apply=%region_3.0 | all-reduce | flops 3584 | bytes 28672 | tf_op jit(solution)/shard_map/psum | solution.py:17
  44.4 3.3 %psum.29 = f32[3584]{0:T(1024)S(1)} all-reduce(f32[3584]{0:T(1024)S(1)} %psum.28), channel_id=1, replica_groups=mesh['section'=2,'dp_0'=2,'dp_1'=2,'shard_0'=4,'shard_1'=8] {'dp_1'}, use_global_device_ids=true, to_apply=%region_4.0 | all-reduce | flops 3584 | bytes 28672 | tf_op jit(solution)/shard_map/psum | solution.py:17
  47.8 17.1 %psum.30 = f32[3584]{0:T(1024)S(1)} all-reduce(f32[3584]{0:T(1024)S(1)} %psum.29), channel_id=1, replica_groups=mesh['section'=2,'dp_0'=2,'dp_1'=2,'shard_0'=4,'shard_1'=8] {'shard_0'}, use_global_device_ids=true, to_apply=%region_5.0 | all-reduce | flops 3584 | bytes 28672 | tf_op jit(solution)/shard_map/psum | solution.py:17
  64.9 32.9 %psum.31 = f32[3584]{0:T(1024)S(1)} all-reduce(f32[3584]{0:T(1024)S(1)} %psum.30), channel_id=1, replica_groups=mesh['section'=2,'dp_0'=2,'dp_1'=2,'shard_0'=4,'shard_1'=8] {'shard_1'}, use_global_device_ids=true, to_apply=%region_6.0 | all-reduce | flops 3584 | bytes 28672 | tf_op jit(solution)/shard_map/psum | solution.py:17
  97.8 0.6 broadcast_in_dim.4
  98.5 3.3 %fusion.12 = bf16[1,1,128,3584]{3,2,1,0:T(8,128)(2,1)} fusion(bf16[1,1,128,3584]{3,2,1,0:T(8,128)(2,1)} %param.8, bf16[1,1,128,3584]{3,2,1,0:T(8,128)(2,1)} %param.7, bf16[1,1,128,3584]{3,2,1,0:T(8,128)(2,1)} %param.5, f32[128]{0:T(128)S(1)} %broadcast_multiply_fusion.1, f32[3584]{0:T(1024)S(1)} %reduce, f32[128]{0:T(128)S(1)} %add_rsqrt_fusion), kind=kLoop, calls=%fused_computation.19 | loop fusion | flops 4587520 | bytes 3685376 | tf_op jit(solution)/shard_map/convert_element_type | solution.py:38
  101.7 146.3 %all-gather.2.cloned.1.call-done = bf16[4096,3584]{1,0:T(8,128)(2,1)} async-done(((bf16[128,3584]{1,0:T(8,128)(2,1)}), bf16[4096,3584]{1,0:T(8,128)(2,1)}) %all-gather.2.cloned.1.call-update) | async-done | bytes 29360144 | tf_op jit(solution)/shard_map/all_gather | solution.py:53
  248.0 0.0 copy-done
  248.0 20.0 %fusion = bf16[1,1,4096,448]{2,3,1,0:T(8,128)(2,1)} fusion(bf16[4096,3584]{1,0:T(8,128)(2,1)} %all-gather.2.cloned.1.call-done, bf16[1,448,3584]{2,1,0:T(8,128)(2,1)S(1)} %copy-done), kind=kOutput, calls=%fused_computation.1 | convolution fusion | flops 13155172352 | bytes 36241408 | tf_op jit(solution)/shard_map/nd,hd->nh/dot_general | solution.py:51
  (3 shorter events, 0.0 us)
Async XLA Ops:
  7.2 240.9 %copy-start = (bf16[1,448,3584]{2,1,0:T(8,128)(2,1)S(1)}, bf16[1,448,3584]{2,1,0:T(8,128)(2,1)}, u32[]{:S(2)}) copy-start(bf16[1,448,3584]{2,1,0:T(8,128)(2,1)} %param.9) | copy-start | bytes 9633796
  7.2 240.8 %all-gather.2.cloned.1.call-start = ((), (), s32[]{:S(2)}) async-start(), calls=%async_computation | async-start | bytes 30277632 | tf_op jit(solution)/shard_map/all_gather | solution.py:53
  9.6 2.3 copy-start.1
  9.6 2.3 copy-start.2
  13.8 22.3 %collective-permute-start = (bf16[128,3584]{1,0:T(8,128)(2,1)S(1)}, bf16[128,3584]{1,0:T(8,128)(2,1)}, u32[]{:S(2)}, u32[]{:S(2)}) collective-permute-start(bf16[128,3584]{1,0:T(8,128)(2,1)S(1)} %fusion.11), channel_id=1, source_target_pairs={{0,128},{128,0},{1,129},{129,1},{2,130},{130,2},{3,131},{131,3},{4... | collective-permute-start | bytes 2752520 | tf_op jit(solution)/shard_map/ppermute | solution.py:28
Sparse Core Ops, SparseCore 0:
  36.2 211.7 all-gather.1
where the time goes:
time: 276 us; the launch traced here: 275 us
  waiting for transfers between devices  167 us (61%)
  blocking collectives  61.8 us (22%)
  matrix products  20 us (7%)
  between operations  14.1 us (5%)
  other arithmetic  9.79 us (4%)
    all_gather x1, waiting for transfers between devices, per_device(): lax.all_gather(arrived, SHARD, axis=0, tiled=True)  146 us
    psum x4, blocking collectives, one_axis_at_a_time(): array = lax.psum(array, axis)  61.8 us
    ppermute x1, waiting for transfers between devices, from_partner(): return lax.ppermute(block, axis, route)  20.9 us
    dot_general x1, matrix products, per_device(): jnp.einsum('nd,hd->nh', lax.all_gather(arrived, SHARD, axis=0, tiled=True...  20 us
  transfers between devices with their start and end apart: 2, of which 2 were waited for; matrix products, arithmetic and copies ran while one was open for 1% of the time, Pallas kernels for 0%

commit v1 on v0

v1 whole, which is shorter than its diff:
```python
import functools

import jax
import jax.numpy as jnp
from jax import lax
from jax.experimental import pallas as pl
from jax.experimental.pallas import tpu as pltpu
from jax.sharding import Mesh
from jax.sharding import PartitionSpec as P

DP_SHARD = ("dp_0", "dp_1", "shard_0", "shard_1")
SHARD = ("shard_0", "shard_1")
DP = ("dp_0", "dp_1")
MESH = pl.DeviceIdType.MESH

epsilon = 1e-05

CHUNKS = 4


def wrap(axis, offset):
    size = lax.axis_size(axis)
    return {axis: lax.rem(lax.axis_index(axis) + (offset % size), size)}


def flip(axis, bit):
    me = lax.axis_index(axis)
    return {axis: me + bit - 2 * bit * lax.rem(me // bit, 2)}


def first_row(rows, hop, way):
    if hop == 0:
        return 0
    if hop == 4:
        return 7 * rows
    return rows * (1 + 2 * (hop - 1) + way)


def kernel(

    input_ref,
    gain_ref,
    branch_ref,
    residual_ref,
    weight_ref,
    boundary_out,
    gain_out,
    unit_out,
    values,
    branch,
    residual,
    boundary,
    acts,
    weight,
    result,
    gain_sum,
    gain_in,
    load_sem,
    own_weight_sem,
    boundary_sem,
    own_result_sem,
    section_send,
    section_recv,
    ring_send,
    ring_recv,
    row_send,
    row_recv,
    core_send,
    core_recv,
    twin_send,
    twin_recv,
    result_send,
    result_recv,
    gain_send,
    gain_recv,
):
    rows, features = input_ref.shape
    units = weight_ref.shape[0]
    quarter = units // 4
    step = rows // CHUNKS
    me_x = lax.axis_index("shard_0")
    me_z = lax.axis_index("shard_1")
    me_twin = lax.axis_index("dp_0")
    me_core = lax.axis_index("dp_1")

    right, left = wrap("shard_1", 1), wrap("shard_1", -1)
    up, down = wrap("shard_0", 1), wrap("shard_0", -1)
    partner, twin, core = wrap("section", 1), wrap("dp_0", 1), wrap("dp_1", 1)
    gain_partners = (
        core,
        twin,
        flip("shard_0", 1),
        wrap("shard_0", 2),
        flip("shard_1", 1),
        flip("shard_1", 2),
        wrap("shard_1", 4),
    )

    def remote(source, target, send, receive, device):
        return pltpu.make_async_remote_copy(
            src_ref=source,
            dst_ref=target,
            send_sem=send,
            recv_sem=receive,
            device_id=device,
            device_id_type=MESH,
        )

    def load(chunk):
        span = pl.ds(pl.multiple_of(chunk * step, step), step)
        return [
            pltpu.make_async_copy(
                ref.at[span], buffer.at[span], load_sem.at[i, chunk]
            )
            for i, (ref, buffer) in enumerate(
                ((input_ref, values), (branch_ref, branch), (residual_ref, residual))
            )
        ]

    @pl.loop(0, CHUNKS)
    def _(chunk):
        for copy in load(chunk):
            copy.start()

    own_weight = pltpu.make_async_copy(weight_ref, weight.at[0], own_weight_sem)
    own_weight.start()

    barrier = pltpu.get_barrier_semaphore()
    others = (
        right,
        left,
        flip("shard_1", 2),
        wrap("shard_1", 4),
        up,
        down,
        wrap("shard_0", 2),
        partner,
        twin,
        core,
    )
    for other in others:
        pl.semaphore_signal(barrier, inc=1, device_id=other, device_id_type=MESH)
    pl.semaphore_wait(barrier, len(others))

    mine = pl.ds(
        pl.multiple_of(me_twin * (2 * quarter) + me_core * quarter, 16), quarter
    )
    theirs = pl.ds(
        pl.multiple_of((1 - me_twin) * (2 * quarter) + me_core * quarter, 16), quarter
    )

    def row_copy(i, source, target, device):
        return remote(source, target, row_send.at[i], row_recv.at[i], device)

    to_up = row_copy(0, weight_ref.at[mine], weight.at[3, mine], up)
    to_down = row_copy(1, weight_ref.at[theirs], weight.at[1, theirs], down)
    pass_up = row_copy(2, weight.at[3, mine], weight.at[2, mine], up)
    pass_down = row_copy(3, weight.at[1, theirs], weight.at[2, theirs], down)
    to_up.start()
    to_down.start()

    def same_place(i, slot, span, device, send, receive):
        piece = weight.at[slot, span]
        return remote(piece, piece, send.at[i], receive.at[i], device)

    to_core = functools.partial(
        same_place, device=core, send=core_send, receive=core_recv
    )
    core_copies = (
        to_core(0, 3, mine),
        to_core(1, 1, theirs),
        to_core(2, 2, mine),
        to_core(3, 2, theirs),
        to_core(4, 3, theirs),
        to_core(5, 1, mine),
    )
    to_twin = functools.partial(
        same_place, device=twin, send=twin_send, receive=twin_recv
    )
    twin_copies = (to_twin(0, 3, mine), to_twin(1, 1, theirs))

    def section_copy(chunk):
        span = pl.ds(pl.multiple_of(chunk * step, step), step)
        return remote(
            boundary.at[span],
            acts.at[span],
            section_send.at[chunk],
            section_recv.at[chunk],
            partner,
        )

    gain_sum[0] = jnp.zeros_like(gain_sum[0])

    @pl.loop(0, CHUNKS)
    def _(chunk):
        for copy in load(chunk):
            copy.wait()
        span = pl.ds(pl.multiple_of(chunk * step, step), step)
        x = values[span, :].astype(jnp.float32)
        inverse = lax.rsqrt(jnp.mean(x * x, axis=-1, keepdims=True) + epsilon)
        normed = x * inverse
        upstream = branch[span, :].astype(jnp.float32)
        scaled = upstream * gain_ref[...]
        project = jnp.mean(scaled * normed, axis=-1, keepdims=True)
        boundary[span, :] = (
            residual[span, :].astype(jnp.float32)
            + inverse * (scaled - normed * project)
        ).astype(boundary.dtype)
        section_copy(chunk).start()
        gain_sum[0] += jnp.sum(upstream * normed, axis=0, keepdims=True)

    boundary_copy = pltpu.make_async_copy(boundary, boundary_out, boundary_sem)
    boundary_copy.start()

    def gain_copy(i):
        return remote(
            gain_sum.at[i],
            gain_in.at[i],
            gain_send.at[i],
            gain_recv.at[i],
            gain_partners[i],
        )

    def gain_step(i):
        gain_copy(i).wait_recv()
        gain_sum[i + 1] = gain_sum[i] + gain_in[i]
        if i + 1 < len(gain_partners):
            gain_copy(i + 1).start()

    gain_copy(0).start()

    def ring_copy(way, hop, chunk):
        here = first_row(rows, hop - 1, way) + chunk * step
        there = first_row(rows, hop, way) + chunk * step
        return remote(
            acts.at[pl.ds(here, step)],
            acts.at[pl.ds(there, step)],
            ring_send.at[way, hop - 1, chunk],
            ring_recv.at[way, hop - 1, chunk],
            (right, left)[way],
        )

    def on_ring(way, hop, chunk):
        return hop < 4 or (hop == 4 and chunk % 2 == way)

    def from_section(chunk):
        section_copy(chunk).wait_recv()
        for way in range(2):
            ring_copy(way, 1, chunk).start()

    def from_ring(hop, chunk):
        for way in range(2):
            if on_ring(way, hop, chunk):
                ring_copy(way, hop, chunk).wait_recv()
                if on_ring(way, hop + 1, chunk):
                    ring_copy(way, hop + 1, chunk).start()

    def tokens_of(origin):
        return pl.ds(pl.multiple_of(me_x * (8 * rows) + origin * rows, rows), rows)

    def result_copy(block, d, origin):
        return remote(
            result.at[d, block],
            unit_out.at[:, tokens_of(origin)],
            result_send.at[d - 1, block],
            result_recv.at[d - 1, block],
            {"shard_0": lax.rem(me_x + d, 4)},
        )

    def own_result_copy(block, origin):
        return pltpu.make_async_copy(
            result.at[0, block],
            unit_out.at[:, tokens_of(origin)],
            own_result_sem.at[block],
        )

    def origins(hop):
        if hop == 0:
            return ((0, me_z),)
        if hop == 4:
            return ((7, lax.rem(me_z + 4, 8)),)
        return (
            (2 * hop - 1, lax.rem(me_z + 8 - hop, 8)),
            (2 * hop, lax.rem(me_z + hop, 8)),
        )

    def product(hop, d):
        blocks = origins(hop)
        found = lax.dot_general(
            weight[d],
            acts[pl.ds(blocks[0][0] * rows, rows * len(blocks)), :],
            (((1,), (1,)), ((), ())),
            preferred_element_type=jnp.float32,
        ).astype(result.dtype)
        for i, (block, _) in enumerate(blocks):
            result[d, block] = found[:, i * rows : (i + 1) * rows]
        return blocks

    def own_product(hop):
        for block, origin in product(hop, 0):
            own_result_copy(block, origin).start()

    def sent_product(hop, d):
        for block, origin in product(hop, d):
            result_copy(block, d, origin).start()

    def side_products(hop):
        @pl.loop(0, 2)
        def _(i):
            sent_product(hop, 1 + 2 * i)

    from_section(0)
    from_section(1)
    gain_step(0)
    from_ring(1, 0)
    from_section(2)
    own_weight.wait()
    from_ring(1, 1)
    to_up.wait_recv()
    pass_up.start()
    core_copies[0].start()
    to_down.wait_recv()
    pass_down.start()
    core_copies[1].start()
    from_section(3)
    twin_copies[0].start()
    twin_copies[1].start()
    gain_step(1)
    own_product(0)
    from_ring(1, 2)
    gain_step(2)
    from_ring(1, 3)
    own_product(1)
    gain_step(3)
    from_ring(2, 0)
    gain_step(4)
    pass_up.wait_recv()
    core_copies[2].start()
    pass_down.wait_recv()
    core_copies[3].start()
    from_ring(2, 1)
    core_copies[2].wait_recv()
    core_copies[3].wait_recv()
    sent_product(0, 2)
    sent_product(1, 2)
    from_ring(2, 2)
    gain_step(5)
    from_ring(2, 3)
    sent_product(2, 2)
    own_product(2)
    gain_step(6)
    gain_out[...] = gain_sum[7] * (1.0 / (32 * rows))
    from_ring(3, 0)
    for i in range(2):
        twin_copies[i].wait_recv()
        core_copies[4 + i].start()
    for i in (0, 1, 4, 5):
        core_copies[i].wait_recv()
    side_products(0)
    from_ring(3, 1)
    side_products(1)
    from_ring(3, 2)
    side_products(2)
    from_ring(3, 3)
    sent_product(3, 2)
    side_products(3)
    own_product(3)
    for chunk in range(CHUNKS):
        from_ring(4, chunk)
    sent_product(4, 2)
    side_products(4)
    own_product(4)

    to_up.wait_send()
    to_down.wait_send()
    pass_up.wait_send()
    pass_down.wait_send()
    for copy in core_copies + twin_copies:
        copy.wait_send()
    for i in range(len(gain_partners)):
        gain_copy(i).wait_send()
    boundary_copy.wait()

    @pl.loop(0, CHUNKS)
    def _(chunk):
        section_copy(chunk).wait_send()

    for way in range(2):
        for hop in range(1, 5):
            for chunk in range(CHUNKS):
                if on_ring(way, hop, chunk):
                    ring_copy(way, hop, chunk).wait_send()
    for hop in range(5):
        for block, origin in origins(hop):
            own_result_copy(block, origin).wait()

    @pl.loop(0, 8)
    def _(block):
        for d in (2, 1, 3):
            copy = result_copy(block, d, 0)
            copy.wait_send()
            copy.wait_recv()


def per_device(norm_input, norm_gain, branch_grad, residual_grad, down_weight):
    rows, features = norm_input.shape[2:]
    units = down_weight.shape[1]
    anywhere = pl.BlockSpec(memory_space=pl.ANY)
    whole = pl.BlockSpec(memory_space=pltpu.VMEM)
    dma = pltpu.SemaphoreType.DMA
    block = pltpu.VMEM((rows, features), jnp.bfloat16)
    boundary, gain_grad, unit_grads = pl.pallas_call(
        kernel,
        out_shape=(
            jax.ShapeDtypeStruct((rows, features), jnp.bfloat16),
            jax.ShapeDtypeStruct((1, features), jnp.float32),
            jax.ShapeDtypeStruct((units, 32 * rows), jnp.bfloat16),
        ),
        in_specs=[anywhere, whole, anywhere, anywhere, anywhere],
        out_specs=(anywhere, whole, anywhere),
        scratch_shapes=[
            block,
            block,
            block,
            block,
            pltpu.VMEM((8 * rows, features), jnp.bfloat16),
            pltpu.VMEM((4, units, features), jnp.bfloat16),
            pltpu.VMEM((4, 8, units, rows), jnp.bfloat16),
            pltpu.VMEM((8, 1, features), jnp.float32),
            pltpu.VMEM((7, 1, features), jnp.float32),
            dma((3, CHUNKS)),
            dma,
            dma,
            dma((8,)),
            dma((CHUNKS,)),
            dma((CHUNKS,)),
            dma((2, 4, CHUNKS)),
            dma((2, 4, CHUNKS)),
            dma((4,)),
            dma((4,)),
            dma((6,)),
            dma((6,)),
            dma((2,)),
            dma((2,)),
            dma((3, 8)),
            dma((3, 8)),
            dma((7,)),
            dma((7,)),
        ],
        compiler_params=pltpu.CompilerParams(
            collective_id=0, has_side_effects=True, vmem_limit_bytes=56 << 20
        ),
        cost_estimate=pl.CostEstimate(
            flops=2 * 8 * rows * 4 * units * features,
            bytes_accessed=16 << 20,
            transcendentals=rows,
        ),
        name="relay_backward",
    )(
        norm_input[0, 0],
        norm_gain,
        branch_grad[0, 0],
        residual_grad[0, 0],
        down_weight[0],
    )
    return (boundary[None, None], gain_grad, unit_grads.T[None, None])


def solution(mesh):
    split = Mesh(
        mesh.devices.reshape(mesh.shape["section"], 2, 2, 4, 8),
        ("section", "dp_0", "dp_1", "shard_0", "shard_1"),
    )
    return jax.shard_map(
        per_device,
        mesh=split,
        in_specs=(
            P("section", DP, SHARD, None),
            P("section", None),
            P("section", DP, SHARD, None),
            P("section", DP, SHARD, None),
            P("section", SHARD, None),
        ),
        out_specs=(
            P("section", DP, SHARD, None),
            P("section", None),
            P("section", DP, None, SHARD),
        ),
        check_vma=False,
    )
```

time: 276 us -> 118 us (0.43)
  waiting for transfers between devices: 167 us -> 0 us
  Pallas kernels: 0 us -> 109 us
  blocking collectives: 61.8 us -> 0 us
  matrix products: 20 us -> 0 us
  between operations: 14.1 us -> 0.64 us
  other arithmetic: 9.79 us -> 0 us
  local copies, waits for them, and re-layouts: 0.63 us -> 7.77 us
    all_gather x1 -> x0, waiting for transfers between devices: 146 us -> none  [per_device(): lax.all_gather(arrived, SHARD, axis=0, tiled=True)]
    pallas_call x0 -> x1, Pallas kernels: none -> 109 us  [per_device(): pl.pallas_call(kernel, out_shape=(jax.ShapeDtypeStruct((rows, features),...]
    psum x4 -> x0, blocking collectives: 61.8 us -> none  [one_axis_at_a_time(): array = lax.psum(array, axis)]
    ppermute x1 -> x0, waiting for transfers between devices: 20.9 us -> none  [from_partner(): return lax.ppermute(block, axis, route)]
    dot_general x1 -> x0, matrix products: 20 us -> none  [per_device(): jnp.einsum('nd,hd->nh', lax.all_gather(arrived, SHARD, axis=0, tiled=True...]
    unnamed x6 -> x3, local copies, waits for them, and re-layouts: 0.02 us -> 7.77 us
    convert_element_type x2 -> x0, other arithmetic: 5.11 us -> none  [norm_backward(): (residual.astype(jnp.float32) + inverse * (scaled - normed * project)).as...]
    reduce_sum x2 -> x0, other arithmetic: 3.91 us -> none  [the longest x1 2.31 us: norm_backward(): return (boundary, jnp.sum(upstream * normed, axis=0))]
  transfers between devices with their start and end apart: 2 -> 0, of which waited for: 2 -> 0; matrix products, arithmetic and copies ran while one was open for 1% -> 0% of each run, Pallas kernels for 0% -> 0%
where the time goes in v1:
time: 118 us; the launch traced here: 117 us
  Pallas kernels  109 us (92%)
  local copies, waits for them, and re-layouts  7.77 us (7%)
    pallas_call x1, Pallas kernels, per_device(): pl.pallas_call(kernel, out_shape=(jax.ShapeDtypeStruct((rows, features),...  109 us
    unnamed x3, local copies, waits for them, and re-layouts  7.77 us

profile of v1, /device:TPU:16, one launch (start us, length us, event | category | flops | bytes accessed | tf_op | source)
XLA Modules:
  0.0 117.3 jit_solution(3089522229902977854)
XLA Ops:
  0.6 108.9 %relay_backward.1 = (bf16[128,3584]{1,0:T(8,128)(2,1)}, f32[1,3584]{1,0:T(1,128)}, bf16[448,4096]{1,0:T(8,128)(2,1)}) custom-call(bf16[128,3584]{1,0:T(8,128)(2,1)} %bitcast.11, f32[1,3584]{1,0:T(1,128)} %gain_ref.1, bf16[128,3584]{1,0:T(8,128)(2,1)} %bitcast.12, bf16[128,3584]{1,0:T(8,128)(2,1)} %bitcast.13, bf16[448,3584]{1,0:T(8,128)(2,1)} %bitcast.10), custom_call_target="tpu_custom_call" | custom-call | flops 13153337344 | bytes 16777216 | tf_op jit(solution)/shard_map/relay_backward/pallas_call | solution.py:412
  109.6 2.2 %copy.11 = bf16[1,1,128,3584]{3,2,1,0:T(8,128)(2,1)} copy(bf16[1,1,128,3584]{3,2,1,0:T(8,128)(2,1)} %bitcast.9) | data formatting | bytes 1835008
  111.7 1.3 %copy.12 = f32[1,3584]{1,0:T(1,128)} copy(f32[1,3584]{1,0:T(1,128)} %get-tuple-element.13) | data formatting | bytes 28672
  113.1 4.3 %copy.13 = bf16[1,1,4096,448]{2,3,1,0:T(8,128)(2,1)} copy(bf16[1,1,4096,448]{2,3,1,0:T(8,128)(2,1)} %bitcast.8) | data formatting | bytes 7340032

commit v2 on v1

v2 whole, which is shorter than its diff:
```python
import functools

import jax
import jax.numpy as jnp
from jax import lax
from jax.experimental import pallas as pl
from jax.experimental.pallas import tpu as pltpu
from jax.sharding import Mesh
from jax.sharding import PartitionSpec as P

DP_SHARD = ("dp_0", "dp_1", "shard_0", "shard_1")
SHARD = ("shard_0", "shard_1")
DP = ("dp_0", "dp_1")
MESH = pl.DeviceIdType.MESH

epsilon = 1e-05

CHUNKS = 8


def wrap(axis, offset):
    size = lax.axis_size(axis)
    return {axis: lax.rem(lax.axis_index(axis) + (offset % size), size)}


def flip(axis, bit):
    me = lax.axis_index(axis)
    return {axis: me + bit - 2 * bit * lax.rem(me // bit, 2)}


def first_row(rows, hop, way):
    if hop == 0:
        return 0
    if hop == 4:
        return 7 * rows
    return rows * (1 + 2 * (hop - 1) + way)


def kernel(
    input_ref,
    gain_ref,
    branch_ref,
    residual_ref,
    weight_ref,
    boundary_out,
    gain_out,
    unit_out,
    values,
    branch,
    residual,
    gain,
    acts,
    weight,
    result,
    gain_sum,
    gain_in,
    load_sem,
    section_recv,
    ring_recv,
    row_recv,
    core_recv,
    twin_recv,
    result_recv,
    gain_recv,
    send_sem,
):
    rows, features = input_ref.shape
    units = weight_ref.shape[0]
    step = rows // CHUNKS
    me_x = lax.axis_index("shard_0")
    me_z = lax.axis_index("shard_1")
    me_twin = lax.axis_index("dp_0")
    me_core = lax.axis_index("dp_1")

    right, left = wrap("shard_1", 1), wrap("shard_1", -1)
    up, down = wrap("shard_0", 1), wrap("shard_0", -1)
    partner, twin, core = wrap("section", 1), wrap("dp_0", 1), wrap("dp_1", 1)
    gain_partners = (
        flip("shard_1", 1),
        flip("shard_1", 2),
        wrap("shard_1", 4),
        core,
        flip("shard_0", 1),
        wrap("shard_0", 2),
        twin,
    )
    by_ring, by_section, by_weight, by_result, by_gain = 0, 2, 3, 4, 7

    def remote(source, target, send, receive, device):
        return pltpu.make_async_remote_copy(
            src_ref=source,
            dst_ref=target,
            send_sem=send_sem.at[send],
            recv_sem=receive,
            device_id=device,
            device_id_type=MESH,
        )

    def take(like, sem):
        pltpu.make_async_copy(like, like, sem).wait()

    def load(start, size, sem):
        span = pl.ds(start, size)
        for ref, buffer in (
            (input_ref, values),
            (branch_ref, branch),
            (residual_ref, residual),
        ):
            pltpu.make_async_copy(ref.at[span], buffer.at[span], sem).start()

    load(0, step, load_sem.at[0])
    gain_load = pltpu.make_async_copy(gain_ref, gain, load_sem.at[2])
    gain_load.start()

    barrier = pltpu.get_barrier_semaphore()
    others = (
        right,
        left,
        flip("shard_1", 2),
        wrap("shard_1", 4),
        up,
        down,
        wrap("shard_0", 2),
        partner,
        twin,
        core,
    )
    for other in others:
        pl.semaphore_signal(barrier, inc=1, device_id=other, device_id_type=MESH)
    load(step, rows - step, load_sem.at[1])
    own_weight = pltpu.make_async_copy(weight_ref, weight.at[0], load_sem.at[3])
    own_weight.start()

    def norm(chunk):
        span = pl.ds(pl.multiple_of(chunk * step, step), step)
        x = values[span, :].astype(jnp.float32)
        inverse = lax.rsqrt(jnp.mean(x * x, axis=-1, keepdims=True) + epsilon)
        normed = x * inverse
        upstream = branch[span, :].astype(jnp.float32)
        scaled = upstream * gain[...]
        project = jnp.mean(scaled * normed, axis=-1, keepdims=True)
        boundary_out[span, :] = (
            residual[span, :].astype(jnp.float32)
            + inverse * (scaled - normed * project)
        ).astype(boundary_out.dtype)
        gain_sum[0] += jnp.sum(upstream * normed, axis=0, keepdims=True)

    def section_copy(chunk):
        span = pl.ds(pl.multiple_of(chunk * step, step), step)
        return remote(
            boundary_out.at[span],
            acts.at[span],
            by_section,
            section_recv.at[chunk],
            partner,
        )

    half = units // 2
    passed = half // 2
    first = (passed // 2 + 15) // 16 * 16
    more = (half // 7 // 16) * 16
    shared = passed - more

    def from_edge(side, near, far, size):
        which = me_twin + side - 2 * me_twin * side
        start = me_core * half + near + which * (far - near)
        return pl.ds(pl.multiple_of(start, 16), size)

    sides = range(2)
    parts = (0, first), (first, passed - first)
    going = [from_edge(side, 0, half - passed, passed) for side in sides]
    going_parts = [
        [from_edge(side, at, half - passed + at, size) for side in sides]
        for at, size in parts
    ]
    extra = [from_edge(side, passed, half - passed - more, more) for side in sides]
    given = [from_edge(side, 0, half - shared, shared) for side in sides]
    gotten = [from_edge(side, half - shared, 0, shared) for side in sides]
    slots = (3, 1)
    ways = (up, down)

    def from_home(i, side, span):
        return remote(
            weight_ref.at[span],
            weight.at[slots[side], span],
            by_weight,
            row_recv.at[i],
            ways[side],
        )

    def onward(i, side, span):
        return remote(
            weight.at[slots[side], span],
            weight.at[2, span],
            by_weight,
            row_recv.at[i],
            ways[side],
        )

    def same_place(slot, span, device, receive):
        there = weight.at[slot, span]
        return remote(there, there, by_weight, receive, device)

    own_copies = [
        [from_home(2 * n + side, side, going_parts[n][side]) for side in sides]
        for n in range(2)
    ]
    extra_copies = [from_home(4 + side, side, extra[side]) for side in sides]
    pass_copies = [
        [onward(6 + 2 * n + side, side, going_parts[n][side]) for side in sides]
        for n in range(2)
    ]
    core_own = [
        same_place(slots[side], going[side], core, core_recv.at[side])
        for side in sides
    ]
    core_extra = [
        same_place(slots[side], extra[side], core, core_recv.at[2 + side])
        for side in sides
    ]
    core_gotten = [
        same_place(slots[side], gotten[side], core, core_recv.at[4 + side])
        for side in sides
    ]
    core_passed = [
        [
            same_place(2, going_parts[n][side], core, core_recv.at[6 + 2 * n + side])
            for side in sides
        ]
        for n in range(2)
    ]
    twin_given = [
        same_place(slots[side], given[side], twin, twin_recv.at[side])
        for side in sides
    ]

    def gain_copy(i):
        return remote(
            gain_sum.at[i], gain_in.at[i], by_gain, gain_recv.at[i], gain_partners[i]
        )

    def gain_step(i):
        gain_copy(i).wait_recv()
        gain_sum[i + 1] = gain_sum[i] + gain_in[i]
        if i + 1 < len(gain_partners):
            gain_copy(i + 1).start()

    def ring_copy(way, hop, chunk):
        here = first_row(rows, hop - 1, way) + chunk * step
        there = first_row(rows, hop, way) + chunk * step
        return remote(
            acts.at[pl.ds(here, step)],
            acts.at[pl.ds(there, step)],
            by_ring + way,
            ring_recv.at[way, hop - 1, chunk],
            (right, left)[way],
        )

    def on_ring(way, hop, chunk):
        return hop < 4 or (hop == 4 and chunk % 2 == way)

    def from_section(chunk):
        section_copy(chunk).wait_recv()
        for way in range(2):
            ring_copy(way, 1, chunk).start()

    def from_ring(hop, *chunks):
        for chunk in chunks:
            for way in range(2):
                if on_ring(way, hop, chunk):
                    ring_copy(way, hop, chunk).wait_recv()
                    if on_ring(way, hop + 1, chunk):
                        ring_copy(way, hop + 1, chunk).start()

    def tokens_of(origin):
        return pl.ds(pl.multiple_of(me_x * (8 * rows) + origin * rows, rows), rows)

    def origins(hop):
        if hop == 0:
            return ((0, me_z),)
        if hop == 4:
            return ((7, lax.rem(me_z + 4, 8)),)
        return (
            (2 * hop - 1, lax.rem(me_z + 8 - hop, 8)),
            (2 * hop, lax.rem(me_z + hop, 8)),
        )

    def product(hop, d):
        blocks = origins(hop)
        return lax.dot_general(
            weight[d],
            acts[pl.ds(blocks[0][0] * rows, rows * len(blocks)), :],
            (((1,), (1,)), ((), ())),
            preferred_element_type=jnp.float32,
        ).astype(result.dtype)

    def own_product(hop):
        found = product(hop, 0)
        for i, (_, origin) in enumerate(origins(hop)):
            unit_out[:, tokens_of(origin)] = found[:, i * rows : (i + 1) * rows]

    def sent_product(hop, d):
        found = product(hop, d)
        for i, (block, origin) in enumerate(origins(hop)):
            result[d - 1, block] = found[:, i * rows : (i + 1) * rows]
            remote(
                result.at[d - 1, block],
                unit_out.at[:, tokens_of(origin)],
                by_result + d - 1,
                result_recv.at[d - 1],
                {"shard_0": lax.rem(me_x + d, 4)},
            ).start()

    def side_products(hop):
        @pl.loop(0, 2)
        def _(i):
            sent_product(hop, 1 + 2 * i)

    gain_sum[0] = jnp.zeros_like(gain_sum[0])
    take(acts.at[pl.ds(0, 3 * step)], load_sem.at[0])
    gain_load.wait()
    norm(0)
    pl.semaphore_wait(barrier, len(others))
    section_copy(0).start()
    for copy in own_copies[0] + own_copies[1]:
        copy.start()
    take(acts.at[pl.ds(0, 3 * (rows - step))], load_sem.at[1])

    @pl.loop(1, CHUNKS)
    def _(chunk):
        norm(chunk)
        section_copy(chunk).start()

    gain_copy(0).start()

    for chunk in range(3):
        from_section(chunk)
    gain_step(0)
    from_section(3)
    from_section(4)
    for side in sides:
        own_copies[0][side].wait_recv()
        pass_copies[0][side].start()
    gain_step(1)
    from_section(5)
    from_section(6)
    from_section(7)
    for side in sides:
        own_copies[1][side].wait_recv()
        pass_copies[1][side].start()
        extra_copies[side].start()
        core_own[side].start()
        twin_given[side].start()
    from_ring(1, 0, 1, 2, 3, 4, 5)
    gain_step(2)
    from_ring(1, 6, 7)
    own_weight.wait()
    own_product(0)
    own_product(1)
    gain_step(3)
    for side in sides:
        pass_copies[0][side].wait_recv()
        core_passed[0][side].start()
    from_ring(2, 0, 1, 2)
    for side in sides:
        pass_copies[1][side].wait_recv()
        core_passed[1][side].start()
    from_ring(2, 3)
    for side in sides:
        core_passed[0][side].wait_recv()
        core_passed[1][side].wait_recv()
    sent_product(0, 2)
    sent_product(1, 2)
    from_ring(2, 4, 5)
    for side in sides:
        extra_copies[side].wait_recv()
        core_extra[side].start()
    gain_step(4)
    from_ring(2, 6, 7)
    sent_product(2, 2)
    for side in sides:
        twin_given[side].wait_recv()
        core_gotten[side].start()
    own_product(2)
    for side in sides:
        core_own[side].wait_recv()
        core_extra[side].wait_recv()
        core_gotten[side].wait_recv()
    side_products(0)
    from_ring(3, 0)
    side_products(1)
    from_ring(3, 1)
    side_products(2)
    gain_step(5)
    from_ring(3, 2, 3, 4, 5, 6, 7)
    sent_product(3, 2)
    side_products(3)
    own_product(3)
    gain_step(6)
    gain_out[...] = gain_sum[7] * (1.0 / (32 * rows))
    from_ring(4, *range(CHUNKS))
    sent_product(4, 2)
    side_products(4)
    own_product(4)

    take(gain_in, send_sem.at[by_gain])
    take(acts.at[pl.ds(0, rows)], send_sem.at[by_section])
    for way in range(2):
        take(acts.at[pl.ds(0, 3 * rows + rows // 2)], send_sem.at[by_ring + way])
    take(weight.at[pl.ds(0, 3)], send_sem.at[by_weight])
    for d in (1, 2, 3):
        take(result.at[d - 1], send_sem.at[by_result + d - 1])
        take(result.at[d - 1], result_recv.at[d - 1])


def per_device(norm_input, norm_gain, branch_grad, residual_grad, down_weight):
    rows, features = norm_input.shape[2:]
    units = down_weight.shape[1]
    anywhere = pl.BlockSpec(memory_space=pl.ANY)
    whole = pl.BlockSpec(memory_space=pltpu.VMEM)
    dma = pltpu.SemaphoreType.DMA
    block = pltpu.VMEM((rows, features), jnp.bfloat16)
    boundary, gain_grad, unit_grads = pl.pallas_call(
        kernel,
        out_shape=(
            block,
            pltpu.VMEM((1, features), jnp.float32),
            pltpu.VMEM((units, 32 * rows), jnp.bfloat16),
        ),
        in_specs=[anywhere] * 5,
        out_specs=(whole,) * 3,
        scratch_shapes=[
            block,
            block,
            block,
            pltpu.VMEM((1, features), jnp.float32),
            pltpu.VMEM((8 * rows, features), jnp.bfloat16),
            pltpu.VMEM((4, units, features), jnp.bfloat16),
            pltpu.VMEM((3, 8, units, rows), jnp.bfloat16),
            pltpu.VMEM((8, 1, features), jnp.float32),
            pltpu.VMEM((7, 1, features), jnp.float32),
            dma((4,)),
            dma((CHUNKS,)),
            dma((2, 4, CHUNKS)),
            dma((10,)),
            dma((10,)),
            dma((2,)),
            dma((3,)),
            dma((7,)),
            dma((8,)),
        ],
        compiler_params=pltpu.CompilerParams(
            collective_id=0, has_side_effects=True, vmem_limit_bytes=54 << 20
        ),
        cost_estimate=pl.CostEstimate(
            flops=2 * 8 * rows * 4 * units * features,
            bytes_accessed=16 << 20,
            transcendentals=rows,
        ),
        name="relay_backward",
    )(
        norm_input[0, 0],
        norm_gain,
        branch_grad[0, 0],
        residual_grad[0, 0],
        down_weight[0],
    )
    return (boundary[None, None], gain_grad, unit_grads.T[None, None])


def solution(mesh):
    split = Mesh(
        mesh.devices.reshape(mesh.shape["section"], 2, 2, 4, 8),
        ("section", "dp_0", "dp_1", "shard_0", "shard_1"),
    )
    return jax.shard_map(
        per_device,
        mesh=split,
        in_specs=(
            P("section", DP, SHARD, None),
            P("section", None),
            P("section", DP, SHARD, None),
            P("section", DP, SHARD, None),
            P("section", SHARD, None),
        ),
        out_specs=(
            P("section", DP, SHARD, None),
            P("section", None),
            P("section", DP, None, SHARD),
        ),
        check_vma=False,
    )
```

time: 118 us -> 97.7 us (0.83)
  Pallas kernels: 109 us -> 93.6 us
  local copies, waits for them, and re-layouts: 7.77 us -> 3.36 us
    pallas_call x1, Pallas kernels: 109 us -> 93.6 us  [per_device(): pl.pallas_call(kernel, out_shape=(block, pltpu.VMEM((1, features), jnp.fl...]
    unnamed x3, local copies, waits for them, and re-layouts: 7.77 us -> 3.36 us
where the time goes in v2:
time: 97.7 us; the launch traced here: 97.6 us
  Pallas kernels  93.6 us (96%)
  local copies, waits for them, and re-layouts  3.36 us (3%)
    pallas_call x1, Pallas kernels, per_device(): pl.pallas_call(kernel, out_shape=(block, pltpu.VMEM((1, features), jnp.fl...  93.6 us
    unnamed x3, local copies, waits for them, and re-layouts  3.36 us

profile of v2, /device:TPU:16, one launch (start us, length us, event | category | flops | bytes accessed | tf_op | source)
XLA Modules:
  0.0 97.6 jit_solution(16408069253448964025)
XLA Ops:
  0.6 93.6 %relay_backward.1 = (bf16[128,3584]{1,0:T(8,128)(2,1)S(1)}, f32[1,3584]{1,0:T(1,128)S(1)}, bf16[448,4096]{1,0:T(8,128)(2,1)S(1)}) custom-call(bf16[128,3584]{1,0:T(8,128)(2,1)} %bitcast.11, f32[1,3584]{1,0:T(1,128)} %gain_ref.1, bf16[128,3584]{1,0:T(8,128)(2,1)} %bitcast.12, bf16[128,3584]{1,0:T(8,128)(2,1)} %bitcast.13, bf16[448,3584]{1,0:T(8,128)(2,1)} %bitcast.10), custom_call_target="tpu_custom_call" | custom-call | flops 13153337344 | bytes 16777216 | tf_op jit(solution)/shard_map/relay_backward/pallas_call | solution.py:423
  94.2 0.9 copy.11
  95.2 0.6 copy.12
  95.8 1.8 %copy.13 = bf16[1,1,4096,448]{2,3,1,0:T(8,128)(2,1)} copy(bf16[1,1,4096,448]{2,3,1,0:T(8,128)(2,1)S(1)} %bitcast.8) | data formatting | bytes 7340032

commit v3 on v2

--- a/solution.py
+++ b/solution.py
@@ -157,7 +157,7 @@
 
     half = units // 2
     passed = half // 2
-    first = (passed // 2 + 15) // 16 * 16
+    first = passed - 16
     more = (half // 7 // 16) * 16
     shared = passed - more
 
@@ -245,32 +245,40 @@
         if i + 1 < len(gain_partners):
             gain_copy(i + 1).start()
 
-    def ring_copy(way, hop, chunk):
-        here = first_row(rows, hop - 1, way) + chunk * step
-        there = first_row(rows, hop, way) + chunk * step
+    pieces = CHUNKS // 2
+
+    def ring_copy(way, hop, piece):
+        size = step if hop == 1 else 2 * step
+        here = first_row(rows, hop - 1, way) + piece * size
+        there = first_row(rows, hop, way) + piece * size
+        index = piece if hop == 1 else CHUNKS + (hop - 2) * pieces + piece
         return remote(
-            acts.at[pl.ds(here, step)],
-            acts.at[pl.ds(there, step)],
+            acts.at[pl.ds(here, size)],
+            acts.at[pl.ds(there, size)],
             by_ring + way,
-            ring_recv.at[way, hop - 1, chunk],
+            ring_recv.at[way, index],
             (right, left)[way],
         )
 
-    def on_ring(way, hop, chunk):
-        return hop < 4 or (hop == 4 and chunk % 2 == way)
+    def on_ring(way, hop, piece):
+        return hop < 4 or (hop == 4 and piece % 2 == way)
 
     def from_section(chunk):
         section_copy(chunk).wait_recv()
         for way in range(2):
             ring_copy(way, 1, chunk).start()
 
-    def from_ring(hop, *chunks):
-        for chunk in chunks:
+    def hear(hop, *some):
+        for piece in some:
             for way in range(2):
-                if on_ring(way, hop, chunk):
-                    ring_copy(way, hop, chunk).wait_recv()
-                    if on_ring(way, hop + 1, chunk):
-                        ring_copy(way, hop + 1, chunk).start()
+                if on_ring(way, hop, piece):
+                    ring_copy(way, hop, piece).wait_recv()
+
+    def pass_on(hop, *some):
+        for piece in some:
+            for way in range(2):
+                if on_ring(way, hop + 1, piece):
+                    ring_copy(way, hop + 1, piece).start()
 
     def tokens_of(origin):
         return pl.ds(pl.multiple_of(me_x * (8 * rows) + origin * rows, rows), rows)
@@ -316,6 +324,11 @@
         def _(i):
             sent_product(hop, 1 + 2 * i)
 
+    def sent_products(hop):
+        @pl.loop(0, 3)
+        def _(i):
+            sent_product(hop, 2 - i + 3 * (i // 2))
+
     gain_sum[0] = jnp.zeros_like(gain_sum[0])
     take(acts.at[pl.ds(0, 3 * step)], load_sem.at[0])
     gain_load.wait()
@@ -338,11 +351,11 @@
     gain_step(0)
     from_section(3)
     from_section(4)
+    gain_step(1)
+    from_section(5)
     for side in sides:
         own_copies[0][side].wait_recv()
         pass_copies[0][side].start()
-    gain_step(1)
-    from_section(5)
     from_section(6)
     from_section(7)
     for side in sides:
@@ -351,56 +364,65 @@
         extra_copies[side].start()
         core_own[side].start()
         twin_given[side].start()
-    from_ring(1, 0, 1, 2, 3, 4, 5)
+    hear(1, 0, 1, 2, 3, 4, 5)
+    pass_on(1, 0, 1, 2)
     gain_step(2)
-    from_ring(1, 6, 7)
+    hear(1, 6, 7)
+    pass_on(1, 3)
     own_weight.wait()
     own_product(0)
     own_product(1)
     gain_step(3)
+    hear(2, 0)
+    pass_on(2, 0)
     for side in sides:
         pass_copies[0][side].wait_recv()
         core_passed[0][side].start()
-    from_ring(2, 0, 1, 2)
+    hear(2, 1)
+    pass_on(2, 1)
     for side in sides:
         pass_copies[1][side].wait_recv()
         core_passed[1][side].start()
-    from_ring(2, 3)
     for side in sides:
         core_passed[0][side].wait_recv()
         core_passed[1][side].wait_recv()
     sent_product(0, 2)
+    hear(2, 2)
+    pass_on(2, 2)
     sent_product(1, 2)
-    from_ring(2, 4, 5)
     for side in sides:
         extra_copies[side].wait_recv()
         core_extra[side].start()
     gain_step(4)
-    from_ring(2, 6, 7)
+    hear(2, 3)
+    pass_on(2, 3)
     sent_product(2, 2)
     for side in sides:
         twin_given[side].wait_recv()
         core_gotten[side].start()
-    own_product(2)
     for side in sides:
         core_own[side].wait_recv()
         core_extra[side].wait_recv()
         core_gotten[side].wait_recv()
     side_products(0)
-    from_ring(3, 0)
+    hear(3, 0)
+    pass_on(3, 0)
     side_products(1)
-    from_ring(3, 1)
+    hear(3, 1)
+    pass_on(3, 1)
     side_products(2)
+    own_product(2)
     gain_step(5)
-    from_ring(3, 2, 3, 4, 5, 6, 7)
-    sent_product(3, 2)
-    side_products(3)
+    hear(3, 2)
+    pass_on(3, 2)
+    hear(3, 3)
+    pass_on(3, 3)
+    sent_products(3)
     own_product(3)
     gain_step(6)
     gain_out[...] = gain_sum[7] * (1.0 / (32 * rows))
-    from_ring(4, *range(CHUNKS))
-    sent_product(4, 2)
-    side_products(4)
+    hear(4, 0, 1, 2, 3)
+    sent_products(4)
     own_product(4)
 
     take(gain_in, send_sem.at[by_gain])
@@ -411,6 +433,22 @@
     for d in (1, 2, 3):
         take(result.at[d - 1], send_sem.at[by_result + d - 1])
         take(result.at[d - 1], result_recv.at[d - 1])
+
+
+def store(boundary_ref, gain_ref, unit_ref, boundary_out, gain_out, unit_out, sem):
+    part = unit_ref.shape[0] // 4
+    pairs = [
+        (unit_ref.at[pl.ds(i * part, part)], unit_out.at[pl.ds(i * part, part)])
+        for i in range(4)
+    ] + [(boundary_ref, boundary_out), (gain_ref, gain_out)]
+    copies = [
+        pltpu.make_async_copy(source, target, sem.at[i])
+        for i, (source, target) in enumerate(pairs)
+    ]
+    for copy in copies:
+        copy.start()
+    for copy in copies:
+        copy.wait()
 
 
 def per_device(norm_input, norm_gain, branch_grad, residual_grad, down_weight):
@@ -441,7 +479,7 @@
             pltpu.VMEM((7, 1, features), jnp.float32),
             dma((4,)),
             dma((CHUNKS,)),
-            dma((2, 4, CHUNKS)),
+            dma((2, CHUNKS + 3 * (CHUNKS // 2))),
             dma((10,)),
             dma((10,)),
             dma((2,)),
@@ -450,7 +488,7 @@
             dma((8,)),
         ],
         compiler_params=pltpu.CompilerParams(
-            collective_id=0, has_side_effects=True, vmem_limit_bytes=54 << 20
+            collective_id=0, has_side_effects=True, vmem_limit_bytes=40 << 20
         ),
         cost_estimate=pl.CostEstimate(
             flops=2 * 8 * rows * 4 * units * features,
@@ -459,11 +497,33 @@
         ),
         name="relay_backward",
     )(
-        norm_input[0, 0],
-        norm_gain,
-        branch_grad[0, 0],
-        residual_grad[0, 0],
-        down_weight[0],
+        *(
+            pltpu.with_memory_space_constraint(given, pltpu.HBM)
+            for given in (
+                norm_input[0, 0],
+                norm_gain,
+                branch_grad[0, 0],
+                residual_grad[0, 0],
+                down_weight[0],
+            )
+        )
+    )
+    boundary, gain_grad, unit_grads = pl.pallas_call(
+        store,
+        out_shape=tuple(
+            jax.ShapeDtypeStruct(found.shape, found.dtype)
+            for found in (boundary, gain_grad, unit_grads)
+        ),
+        in_specs=[whole] * 3,
+        out_specs=(anywhere,) * 3,
+        scratch_shapes=[dma((6,))],
+        compiler_params=pltpu.CompilerParams(vmem_limit_bytes=1 << 20),
+        name="store_results",
+    )(
+        *(
+            pltpu.with_memory_space_constraint(found, pltpu.VMEM)
+            for found in (boundary, gain_grad, unit_grads)
+        )
     )
     return (boundary[None, None], gain_grad, unit_grads.T[None, None])
 

time: 97.7 us -> 95.6 us (0.979)
  local copies, waits for them, and re-layouts: 3.36 us -> 0 us
  Pallas kernels: 93.6 us -> 94.9 us
    unnamed x3 -> x0, local copies, waits for them, and re-layouts: 3.36 us -> none
    pallas_call x0 -> x1, Pallas kernels: none -> 2.19 us  [per_device(): pl.pallas_call(store, out_shape=tuple((jax.ShapeDtypeStruct(found.shape,...]
where the time goes in v3:
time: 95.6 us; the launch traced here: 95.5 us
  Pallas kernels  94.9 us (99%)
    pallas_call x1, Pallas kernels, per_device(): pl.pallas_call(kernel, out_shape=(block, pltpu.VMEM((1, features), jnp.fl...  92.7 us
    pallas_call x1, Pallas kernels, per_device(): pl.pallas_call(store, out_shape=tuple((jax.ShapeDtypeStruct(found.shape,...  2.19 us

profile of v3, /device:TPU:16, one launch (start us, length us, event | category | flops | bytes accessed | tf_op | source)
XLA Modules:
  0.0 95.5 jit_solution(17420348953654230414)
XLA Ops:
  0.6 92.7 %relay_backward.1 = (bf16[128,3584]{1,0:T(8,128)(2,1)S(1)}, f32[1,3584]{1,0:T(1,128)S(1)}, bf16[448,4096]{1,0:T(8,128)(2,1)S(1)}) custom-call(bf16[128,3584]{1,0:T(8,128)(2,1)} %bitcast.10, f32[1,3584]{1,0:T(1,128)} %gain_ref.1, bf16[128,3584]{1,0:T(8,128)(2,1)} %bitcast.11, bf16[128,3584]{1,0:T(8,128)(2,1)} %bitcast.12, bf16[448,3584]{1,0:T(8,128)(2,1)} %bitcast.9), custom_call_target="tpu_custom_call" | custom-call | flops 13153337344 | bytes 16777216 | tf_op jit(solution)/shard_map/relay_backward/pallas_call | solution.py:461
  93.3 2.2 %store_results.1 = (bf16[128,3584]{1,0:T(8,128)(2,1)}, f32[1,3584]{1,0:T(1,128)}, bf16[448,4096]{1,0:T(8,128)(2,1)}) custom-call(bf16[128,3584]{1,0:T(8,128)(2,1)S(1)} %get-tuple-element.9.boundary_ref, f32[1,3584]{1,0:T(1,128)S(1)} %get-tuple-element.10.gain_ref, bf16[448,4096]{1,0:T(8,128)(2,1)S(1)} %get-tuple-element.11.unit_ref), custom_call_target="tpu_custom_call" | custom-call | tf_op jit(solution)/shard_map/store_results/pallas_call | solution.py:511

commit v4 on v3

--- a/solution.py
+++ b/solution.py
@@ -202,37 +202,40 @@
         return remote(there, there, by_weight, receive, device)
 
     own_copies = [
-        [from_home(2 * n + side, side, going_parts[n][side]) for side in sides]
+        [from_home(n, side, going_parts[n][side]) for side in sides]
         for n in range(2)
     ]
-    extra_copies = [from_home(4 + side, side, extra[side]) for side in sides]
+    extra_copies = [from_home(2, side, extra[side]) for side in sides]
     pass_copies = [
-        [onward(6 + 2 * n + side, side, going_parts[n][side]) for side in sides]
+        [onward(3 + n, side, going_parts[n][side]) for side in sides]
         for n in range(2)
     ]
     core_own = [
-        same_place(slots[side], going[side], core, core_recv.at[side])
+        same_place(slots[side], going[side], core, core_recv.at[0])
         for side in sides
     ]
     core_extra = [
-        same_place(slots[side], extra[side], core, core_recv.at[2 + side])
+        same_place(slots[side], extra[side], core, core_recv.at[1])
         for side in sides
     ]
     core_gotten = [
-        same_place(slots[side], gotten[side], core, core_recv.at[4 + side])
+        same_place(slots[side], gotten[side], core, core_recv.at[2])
         for side in sides
     ]
     core_passed = [
         [
-            same_place(2, going_parts[n][side], core, core_recv.at[6 + 2 * n + side])
+            same_place(2, going_parts[n][side], core, core_recv.at[3 + n])
             for side in sides
         ]
         for n in range(2)
     ]
     twin_given = [
-        same_place(slots[side], given[side], twin, twin_recv.at[side])
+        same_place(slots[side], given[side], twin, twin_recv.at[0])
         for side in sides
     ]
+
+    def both(size, sem):
+        take(acts.at[pl.ds(0, 2 * size)], sem)
 
     def gain_copy(i):
         return remote(
@@ -247,16 +250,19 @@
 
     pieces = CHUNKS // 2
 
+    def ring_index(hop, piece):
+        return piece if hop == 1 else CHUNKS + (hop - 2) * pieces + piece
+
     def ring_copy(way, hop, piece):
         size = step if hop == 1 else 2 * step
         here = first_row(rows, hop - 1, way) + piece * size
         there = first_row(rows, hop, way) + piece * size
-        index = piece if hop == 1 else CHUNKS + (hop - 2) * pieces + piece
+        index = ring_index(hop, piece)
         return remote(
             acts.at[pl.ds(here, size)],
             acts.at[pl.ds(there, size)],
             by_ring + way,
-            ring_recv.at[way, index],
+            ring_recv.at[index],
             (right, left)[way],
         )
 
@@ -269,10 +275,13 @@
             ring_copy(way, 1, chunk).start()
 
     def hear(hop, *some):
+        size = step if hop == 1 else 2 * step
         for piece in some:
-            for way in range(2):
-                if on_ring(way, hop, piece):
-                    ring_copy(way, hop, piece).wait_recv()
+            arrive = sum(on_ring(way, hop, piece) for way in range(2))
+            take(
+                acts.at[pl.ds(0, arrive * size)],
+                ring_recv.at[ring_index(hop, piece)],
+            )
 
     def pass_on(hop, *some):
         for piece in some:
@@ -353,13 +362,13 @@
     from_section(4)
     gain_step(1)
     from_section(5)
+    both(first, row_recv.at[0])
     for side in sides:
-        own_copies[0][side].wait_recv()
         pass_copies[0][side].start()
     from_section(6)
     from_section(7)
+    both(passed - first, row_recv.at[1])
     for side in sides:
-        own_copies[1][side].wait_recv()
         pass_copies[1][side].start()
         extra_copies[side].start()
         core_own[side].start()
@@ -375,35 +384,33 @@
     gain_step(3)
     hear(2, 0)
     pass_on(2, 0)
+    both(first, row_recv.at[3])
     for side in sides:
-        pass_copies[0][side].wait_recv()
         core_passed[0][side].start()
     hear(2, 1)
     pass_on(2, 1)
+    both(passed - first, row_recv.at[4])
     for side in sides:
-        pass_copies[1][side].wait_recv()
         core_passed[1][side].start()
-    for side in sides:
-        core_passed[0][side].wait_recv()
-        core_passed[1][side].wait_recv()
+    both(first, core_recv.at[3])
+    both(passed - first, core_recv.at[4])
     sent_product(0, 2)
     hear(2, 2)
     pass_on(2, 2)
     sent_product(1, 2)
+    both(more, row_recv.at[2])
     for side in sides:
-        extra_copies[side].wait_recv()
         core_extra[side].start()
     gain_step(4)
     hear(2, 3)
     pass_on(2, 3)
     sent_product(2, 2)
+    both(shared, twin_recv.at[0])
     for side in sides:
-        twin_given[side].wait_recv()
         core_gotten[side].start()
-    for side in sides:
-        core_own[side].wait_recv()
-        core_extra[side].wait_recv()
-        core_gotten[side].wait_recv()
+    both(passed, core_recv.at[0])
+    both(more, core_recv.at[1])
+    both(shared, core_recv.at[2])
     side_products(0)
     hear(3, 0)
     pass_on(3, 0)
@@ -479,10 +486,10 @@
             pltpu.VMEM((7, 1, features), jnp.float32),
             dma((4,)),
             dma((CHUNKS,)),
-            dma((2, CHUNKS + 3 * (CHUNKS // 2))),
-            dma((10,)),
-            dma((10,)),
-            dma((2,)),
+            dma((CHUNKS + 3 * (CHUNKS // 2),)),
+            dma((5,)),
+            dma((5,)),
+            dma((1,)),
             dma((3,)),
             dma((7,)),
             dma((8,)),

time: 95.6 us -> 95.3 us (level)
  no operation moved by 1% of the time
where the time goes in v4:
time: 95.3 us; the launch traced here: 95.2 us
  Pallas kernels  94.6 us (99%)
    pallas_call x1, Pallas kernels, per_device(): pl.pallas_call(kernel, out_shape=(block, pltpu.VMEM((1, features), jnp.fl...  92.4 us
    pallas_call x1, Pallas kernels, per_device(): pl.pallas_call(store, out_shape=tuple((jax.ShapeDtypeStruct(found.shape,...  2.19 us

profile of v4, /device:TPU:16, one launch (start us, length us, event | category | flops | bytes accessed | tf_op | source)
XLA Modules:
  0.0 95.2 jit_solution(5352174790874173472)
XLA Ops:
  0.6 92.4 %relay_backward.1 = (bf16[128,3584]{1,0:T(8,128)(2,1)S(1)}, f32[1,3584]{1,0:T(1,128)S(1)}, bf16[448,4096]{1,0:T(8,128)(2,1)S(1)}) custom-call(bf16[128,3584]{1,0:T(8,128)(2,1)} %bitcast.10, f32[1,3584]{1,0:T(1,128)} %gain_ref.1, bf16[128,3584]{1,0:T(8,128)(2,1)} %bitcast.11, bf16[128,3584]{1,0:T(8,128)(2,1)} %bitcast.12, bf16[448,3584]{1,0:T(8,128)(2,1)} %bitcast.9), custom_call_target="tpu_custom_call" | custom-call | flops 13153337344 | bytes 16777216 | tf_op jit(solution)/shard_map/relay_backward/pallas_call | solution.py:468
  93.0 2.2 %store_results.1 = (bf16[128,3584]{1,0:T(8,128)(2,1)}, f32[1,3584]{1,0:T(1,128)}, bf16[448,4096]{1,0:T(8,128)(2,1)}) custom-call(bf16[128,3584]{1,0:T(8,128)(2,1)S(1)} %get-tuple-element.9.boundary_ref, f32[1,3584]{1,0:T(1,128)S(1)} %get-tuple-element.10.gain_ref, bf16[448,4096]{1,0:T(8,128)(2,1)S(1)} %get-tuple-element.11.unit_ref), custom_call_target="tpu_custom_call" | custom-call | tf_op jit(solution)/shard_map/store_results/pallas_call | solution.py:518
